TPU v7x, 256 devices: a whole 4x4x8 slice. The times are simulated.
256 devices in a mesh: gx: 16 (over z_lo, x), gy: 16 (over y, z_hi, core).
Axes of the slice: x: 4, y: 4, z: 8 (z_hi: 2, z_lo: 4; z = z_hi * 4 + z_lo), core: 2. Of those that a mesh axis runs over, the one named last changes fastest.
Arguments:
- features: float32 [16, 128, 256, 128], P(None, 'gx', 'gy'), may hold values from -6 to 6
- conv_weight: float32 [27, 16, 16], replicated, may hold values from -0.3125 to 0.3125
- mix_weight: float32 [2, 16, 16, 16, 432], P(None, None, None, 'gy', 'gx'), may hold values from -1 to 1
Outputs:
- layer_out: float32 [16, 128, 256, 128], P(None, 'gx', 'gy')
All inputs are finite; a program needn't handle non-finite values.
Results may differ from a plain program's by a relative error of at most 0.0001.
Values sent between devices are 32-bit elements; how exact they have to be, the bound alone decides.
A program may use at most 128 MiB of HBM per device.

v0:
```python
import math
import jax
import jax.numpy as jnp
from jax import lax
from jax.sharding import PartitionSpec as P

KX = 24
KY = 24
KZ = 12
PRECISE = lax.Precision.HIGHEST


def padded_2(array, sides, width):
    for axis, dim in sides:
        size, length = (lax.axis_size(axis), array.shape[dim])
        up = [(i, (i + 1) % size) for i in range(size)]
        down = [(j, i) for i, j in up]
        last = lax.slice_in_dim(array, length - width, length, axis=dim)
        initial = lax.slice_in_dim(array, 0, width, axis=dim)
        before = lax.ppermute(last, axis, up)
        after = lax.ppermute(initial, axis, down)
        array = jnp.concatenate([before, array, after], axis=dim)
    return array


def angle_tables(positions, frequencies, length):
    product = positions[:, None] * frequencies[None, :] % length
    angles = product.astype(jnp.float32) * (2.0 * math.pi / length)
    return (jnp.cos(angles), jnp.sin(angles))


def kept_frequencies(amount, length):
    index = jnp.arange(amount, dtype=jnp.int32)
    return jnp.where(index < amount // 2, index, length - amount + index)


def forward_x(part_real, part_imag, cos_x, sin_x):
    out_real = jnp.einsum("cxm,xp->cpm", part_real, cos_x, precision=PRECISE) + jnp.einsum(
        "cxm,xp->cpm", part_imag, sin_x, precision=PRECISE
    )
    out_imag = jnp.einsum("cxm,xp->cpm", part_imag, cos_x, precision=PRECISE) - jnp.einsum(
        "cxm,xp->cpm", part_real, sin_x, precision=PRECISE
    )
    return (out_real, out_imag)


def inverse_x(part_real, part_imag, cos_x, sin_x):
    out_real = jnp.einsum("cpm,xp->cxm", part_real, cos_x, precision=PRECISE) - jnp.einsum(
        "cpm,xp->cxm", part_imag, sin_x, precision=PRECISE
    )
    out_imag = jnp.einsum("cpm,xp->cxm", part_imag, cos_x, precision=PRECISE) + jnp.einsum(
        "cpm,xp->cxm", part_real, sin_x, precision=PRECISE
    )
    return (out_real, out_imag)


def shards(features, conv_weight, mix_weight):
    channels, cells_x, cells_y, length_z = features.shape
    count_gx = lax.axis_size("gx")
    count_gy = lax.axis_size("gy")
    length_x = cells_x * count_gx
    length_y = cells_y * count_gy
    block_yz = KY * KZ // count_gy
    padded = padded_2(features, (("gx", 1), ("gy", 2)), 1)
    wrapped = jnp.concatenate([padded[..., -1:], padded, padded[..., :1]], axis=3)
    kernel = conv_weight.reshape(3, 3, 3, channels, channels).transpose(3, 4, 0, 1, 2)
    conv_sum = lax.conv_general_dilated(
        wrapped[None],
        kernel,
        (1, 1, 1),
        "VALID",
        dimension_numbers=("NCDHW", "OIDHW", "NCDHW"),
        precision=PRECISE,
    )[0]
    cos_z, sin_z = angle_tables(
        jnp.arange(length_z, dtype=jnp.int32), jnp.arange(KZ, dtype=jnp.int32), length_z
    )
    y_places = lax.axis_index("gy") * cells_y + jnp.arange(cells_y, dtype=jnp.int32)
    x_places = lax.axis_index("gx") * cells_x + jnp.arange(cells_x, dtype=jnp.int32)
    cos_y, sin_y = angle_tables(y_places, kept_frequencies(KY, length_y), length_y)
    cos_x, sin_x = angle_tables(x_places, kept_frequencies(KX, length_x), length_x)
    table_z = jnp.concatenate([cos_z, -sin_z], axis=1)
    along_z = jnp.dot(features, table_z, precision=PRECISE)
    z_real = along_z[..., :KZ]
    z_imag = along_z[..., KZ:]
    y_real = jnp.einsum("cxyk,yq->cxqk", z_real, cos_y, precision=PRECISE) + jnp.einsum(
        "cxyk,yq->cxqk", z_imag, sin_y, precision=PRECISE
    )
    y_imag = jnp.einsum("cxyk,yq->cxqk", z_imag, cos_y, precision=PRECISE) - jnp.einsum(
        "cxyk,yq->cxqk", z_real, sin_y, precision=PRECISE
    )
    partial_value = jnp.stack([y_real, y_imag], axis=2).reshape(channels, cells_x, 2, KY * KZ)
    y_share = lax.psum_scatter(partial_value, "gy", scatter_dimension=3, tiled=True)
    x_real, x_imag = forward_x(y_share[:, :, 0], y_share[:, :, 1], cos_x, sin_x)
    x_partial = jnp.stack([x_real, x_imag], axis=1).reshape(channels, 2, KX * block_yz)
    owned_modes = lax.psum_scatter(x_partial, "gx", scatter_dimension=2, tiled=True)
    forward_scale = 1.0 / math.sqrt(length_x * length_y * length_z)
    owned_modes = owned_modes * forward_scale
    coef_real = owned_modes[:, 0]
    coef_imag = owned_modes[:, 1]
    weight_real = mix_weight[0, :, :, 0, :]
    weight_imag = mix_weight[1, :, :, 0, :]
    mixed_real = jnp.einsum("oim,im->om", weight_real, coef_real, precision=PRECISE) - jnp.einsum(
        "oim,im->om", weight_imag, coef_imag, precision=PRECISE
    )
    mixed_imag = jnp.einsum("oim,im->om", weight_real, coef_imag, precision=PRECISE) + jnp.einsum(
        "oim,im->om", weight_imag, coef_real, precision=PRECISE
    )
    mixed_modes = jnp.stack([mixed_real, mixed_imag], axis=1)
    row_modes = lax.all_gather(mixed_modes, "gx", axis=2, tiled=True).reshape(
        channels, 2, KX, block_yz
    )
    back_real, back_imag = inverse_x(row_modes[:, 0], row_modes[:, 1], cos_x, sin_x)
    x_inverse = jnp.stack([back_real, back_imag], axis=2)
    gathered = lax.all_gather(x_inverse, "gy", axis=3, tiled=True)
    back_real = gathered[:, :, 0].reshape(channels, cells_x, KY, KZ)
    back_imag = gathered[:, :, 1].reshape(channels, cells_x, KY, KZ)
    plane_real = jnp.einsum("cxqk,yq->cxyk", back_real, cos_y, precision=PRECISE) - jnp.einsum(
        "cxqk,yq->cxyk", back_imag, sin_y, precision=PRECISE
    )
    plane_imag = jnp.einsum("cxqk,yq->cxyk", back_imag, cos_y, precision=PRECISE) + jnp.einsum(
        "cxqk,yq->cxyk", back_real, sin_y, precision=PRECISE
    )
    table_back = jnp.concatenate([cos_z.T, -sin_z.T], axis=0)
    inverse_scale = 1.0 / math.sqrt(KX * KY * KZ)
    spectral = (
        jnp.dot(jnp.concatenate([plane_real, plane_imag], axis=3), table_back, precision=PRECISE)
        * inverse_scale
    )
    return jax.nn.gelu(conv_sum + spectral, approximate=False)


def solution(mesh):
    in_specs = (P(None, "gx", "gy", None), P(), P(None, None, None, "gy", "gx"))
    out_specs = P(None, "gx", "gy", None)
    return jax.shard_map(shards, mesh=mesh, in_specs=in_specs, out_specs=out_specs, check_vma=False)
```

profile of v0, /device:TPU:7, one launch (start us, length us, event | category | flops | bytes accessed | tf_op | source)
XLA Modules:
  0.0 493.7 jit_solution(6698932705271622397)
XLA Ops:
  6.6 2.2 convolution_bitcast_fusion
  8.8 1.3 fusion.181
  10.1 2.1 copy.51
  14.9 1.8 fusion.13
  16.7 2.0 copy.53
  22.3 1.6 collective-permute-start
  27.6 2.3 collective-permute-done.1
  30.0 8.1 %collective-permute-start.2 = (f32[16,10,1,128]{3,0,2,1:T(8,128)S(1)}, f32[16,10,1,128]{3,0,2,1:T(8,128)S(1)}, u32[]{:S(2)}, u32[]{:S(2)}) collective-permute-start(f32[16,10,1,128]{3,0,2,1:T(8,128)S(1)} %get-tuple-element.15), channel_id=1, source_target_pairs={{0,1},{1,2},{2,3},{3,4},{4,5},{5,6},{6,7},{7,8},{8,9},{9,10},{10,1... | collective-permute-start | bytes 245768 | tf_op jit(solution)/shard_map/ppermute | solution.py:20
  39.5 7.2 %collective-permute-done.3 = f32[16,10,1,128]{3,0,2,1:T(8,128)S(1)} collective-permute-done((f32[16,10,1,128]{3,0,2,1:T(8,128)S(1)}, f32[16,10,1,128]{3,0,2,1:T(8,128)S(1)}, u32[]{:S(2)}, u32[]{:S(2)}) %collective-permute-start.3) | collective-permute-done | bytes 81952 | tf_op jit(solution)/shard_map/ppermute | solution.py:21
  47.3 1.2 maximum_bitcast_fusion
  48.9 6.5 %reshape.44 = f32[16,10,18,1,8,17]{5,4,0,2,1,3:T(8,128)} reshape(f32[16,10,18,1,136]{4,0,2,1,3:T(8,128)S(1)} %pad) | data formatting | bytes 3133440 | tf_op jit(solution)/shard_map/conv_general_dilated | solution.py:67
  55.4 15.0 %copy.47 = f32[16,10,18,1,8,17]{0,4,5,2,1,3:T(8,128)} copy(f32[16,10,18,1,8,17]{5,4,0,2,1,3:T(8,128)} %reshape.44) | data formatting | bytes 3133440 | tf_op jit(solution)/shard_map/conv_general_dilated | solution.py:67
  70.4 1.5 slice.80
  71.9 5.3 %fusion.197 = f32[16,10,18,8,19]{0,3,4,2,1:T(8,128)S(1)} fusion(f32[16,10,18,1,7,2]{0,4,5,2,1,3:T(8,128)S(1)} %slice.80, f32[16,10,18,1,8,17]{0,4,5,2,1,3:T(8,128)} %copy.47), kind=kLoop, calls=%fused_computation.1.clone.clone.clone.clone.1 | loop fusion | flops 1313280 | bytes 3479040 | tf_op jit(solution)/shard_map/conv_general_dilated | solution.py:67
  77.2 193.4 %broadcast_select_fusion = f32[8,16,8,17,16]{4,2,3,1,0:T(8,128)} fusion(pred[8,17]{0,1:T(8,128)(4,1)S(1)} %copy-done.7, f32[3,3,3,16,16]{4,3,2,1,0:T(8,128)S(1)} %bitcast.181, f32[16,10,18,8,19]{0,3,4,2,1:T(8,128)S(1)} %fusion.197), kind=kOutput, calls=%fused_computation.8 | convolution fusion | flops 1444167680 | bytes 2892936 | tf_op jit(solution)/shard_map/conv_general_dilated | solution.py:67
  270.7 12.7 %copy.98 = f32[8,16,8,17,16]{3,2,1,0,4:T(8,128)} copy(f32[8,16,8,17,16]{4,2,3,1,0:T(8,128)} %broadcast_select_fusion) | data formatting | bytes 2228224 | tf_op jit(solution)/shard_map/conv_general_dilated | solution.py:67
  283.4 7.0 %reshape.68 = f32[8,16,1,136,16]{3,1,0,4,2:T(8,128)} reshape(f32[8,16,8,17,16]{3,2,1,0,4:T(8,128)} %copy.98) | data formatting | bytes 2228224 | tf_op jit(solution)/shard_map/conv_general_dilated | solution.py:67
  290.4 1.4 fusion.38
  291.8 1.4 fusion.15
  293.3 1.4 fusion.39
  294.7 1.4 fusion.14
  296.3 57.2 %all-reduce.1 = f32[16,2,432]{2,0,1:T(8,128)S(1)} all-reduce(f32[16,2,432]{2,0,1:T(8,128)S(1)} %pad_maximum_fusion.3), channel_id=3, replica_groups=mesh['gx'=16,'gy'=16] {'gx'}, use_global_device_ids=true, to_apply=%region_1.2.clone | all-reduce | flops 13824 | bytes 110592
  353.8 38.1 %all_gather.6 = f32[16,2,432]{0,1,2:T(2,128)S(1)} all-gather(f32[16,2,27]{0,1,2:T(2,128)S(1)} %copy.57), channel_id=1, replica_groups=mesh['gx'=16,'gy'=16] {'gx'}, dimensions={2}, use_global_device_ids=true | all-gather | bytes 58752 | tf_op jit(solution)/shard_map/all_gather | solution.py:110
  394.2 76.2 %all_gather.7 = f32[16,8,2,288]{0,1,2,3:T(8,128)S(1)} all-gather(f32[16,8,2,18]{0,1,2,3:T(8,128)S(1)} %copy.59), channel_id=1, replica_groups=mesh['gx'=16,'gy'=16] {'gy'}, dimensions={3}, use_global_device_ids=true | all-gather | bytes 313344 | tf_op jit(solution)/shard_map/all_gather | solution.py:115
  470.4 1.2 fusion.177
  471.5 1.7 copy.93
  473.2 2.2 fusion.59
  475.4 2.9 copy.94
  478.3 1.2 fusion.57
  479.5 1.2 fusion.10
  480.7 1.2 fusion.9
  482.3 4.2 fusion.19
  (70 shorter events, 14.2 us)
Async XLA Ops:
  6.5 283.9 %all-reduce.4.cloned.1.call-start = ((), (), s32[]{:S(2)}) async-start(), calls=%async_computation | async-start | bytes 786432
  20.8 1.3 copy-start
  21.3 2.7 copy-start.3
  21.3 2.8 copy-start.6
  21.3 3.4 copy-start.5
  21.4 4.0 copy-start.4
  22.3 4.7 collective-permute-start
  23.9 6.0 %collective-permute-start.1 = (f32[16,1,16,128]{3,0,2,1:T(8,128)S(1)}, f32[16,1,16,128]{3,0,2,1:T(8,128)S(1)}, u32[]{:S(2)}, u32[]{:S(2)}) collective-permute-start(f32[16,1,16,128]{3,0,2,1:T(8,128)S(1)} %copy.121), channel_id=1, source_target_pairs={{16,0},{32,16},{48,32},{64,48},{80,64},{96,80},{112,96},{128,112},... | collective-permute-start | bytes 393224 | tf_op jit(solution)/shard_map/ppermute | solution.py:21
  30.0 9.6 %collective-permute-start.2 = (f32[16,10,1,128]{3,0,2,1:T(8,128)S(1)}, f32[16,10,1,128]{3,0,2,1:T(8,128)S(1)}, u32[]{:S(2)}, u32[]{:S(2)}) collective-permute-start(f32[16,10,1,128]{3,0,2,1:T(8,128)S(1)} %get-tuple-element.15), channel_id=1, source_target_pairs={{0,1},{1,2},{2,3},{3,4},{4,5},{5,6},{6,7},{7,8},{8,9},{9,10},{10,1... | collective-permute-start | bytes 245768 | tf_op jit(solution)/shard_map/ppermute | solution.py:20
  38.1 8.7 %collective-permute-start.3 = (f32[16,10,1,128]{3,0,2,1:T(8,128)S(1)}, f32[16,10,1,128]{3,0,2,1:T(8,128)S(1)}, u32[]{:S(2)}, u32[]{:S(2)}) collective-permute-start(f32[16,10,1,128]{3,0,2,1:T(8,128)S(1)} %get-tuple-element.16), channel_id=1, source_target_pairs={{1,0},{2,1},{3,2},{4,3},{5,4},{6,5},{7,6},{8,7},{9,8},{10,9},{11,1... | collective-permute-start | bytes 245768 | tf_op jit(solution)/shard_map/ppermute | solution.py:21
  71.9 5.3 %copy-start.7 = (pred[8,17]{0,1:T(8,128)(4,1)S(1)}, pred[8,17]{0,1:T(8,128)(4,1)}, u32[]{:S(2)}) copy-start(pred[8,17]{0,1:T(8,128)(4,1)} %constant.131) | copy-start | bytes 412
  478.3 1.2 copy-start.1
  480.7 1.6 copy-start.2
Sparse Core Ops, SparseCore 0:
  22.3 182.2 all-reduce.3
where the time goes:
time: 503 us; the launch traced here: 494 us
  matrix products  217 us (43%)
  blocking collectives  171 us (34%)
  local copies, waits for them, and re-layouts  61.4 us (12%)
  between operations  15.6 us (3%)
  waiting for transfers between devices  10.6 us (2%)
  starting transfers between devices  10.2 us (2%)
  other arithmetic  7.72 us (2%)
    conv_general_dilated x1, matrix products, shards(): lax.conv_general_dilated(wrapped[None], kernel, (1, 1, 1), 'VALID', dimen...  193 us
    all_gather x1, blocking collectives, shards(): gathered = lax.all_gather(x_inverse, 'gy', axis=3, tiled=True)  76.2 us
    unnamed x1, blocking collectives  57.2 us
    conv_general_dilated x5, local copies, waits for them, and re-layouts, shards(): lax.conv_general_dilated(wrapped[None], kernel, (1, 1, 1), 'VALID', dimen...  42.8 us
    all_gather x1, blocking collectives, shards(): lax.all_gather(mixed_modes, 'gx', axis=2, tiled=True)  38.1 us
  transfers between devices with their start and end apart: 5, of which 3 were waited for; matrix products, arithmetic and copies ran while one was open for 50% of the time, Pallas kernels for 0%

commit v1 on v0

--- a/solution.py
+++ b/solution.py
@@ -112,7 +112,9 @@
     )
     back_real, back_imag = inverse_x(row_modes[:, 0], row_modes[:, 1], cos_x, sin_x)
     x_inverse = jnp.stack([back_real, back_imag], axis=2)
-    gathered = lax.all_gather(x_inverse, "gy", axis=3, tiled=True)
+    gathered = jnp.concatenate(
+        lax.all_to_all(jnp.stack([x_inverse] * lax.axis_size("gy")), "gy", 0, 0), axis=3
+    )
     back_real = gathered[:, :, 0].reshape(channels, cells_x, KY, KZ)
     back_imag = gathered[:, :, 1].reshape(channels, cells_x, KY, KZ)
     plane_real = jnp.einsum("cxqk,yq->cxyk", back_real, cos_y, precision=PRECISE) - jnp.einsum(

time: 503 us -> 607 us (1.21)
  the two profiles are of different devices: /device:TPU:7 before, /device:TPU:1 now
where the time goes in v1:
time: 607 us; the launch traced here: 597 us
  matrix products  237 us (39%)
  waiting for transfers between devices  130 us (21%)
  blocking collectives  94.9 us (16%)
  local copies, waits for them, and re-layouts  64.3 us (11%)
  starting transfers between devices  42.4 us (7%)
  between operations  15.5 us (3%)
  other arithmetic  13.5 us (2%)
    conv_general_dilated x1, matrix products, shards(): lax.conv_general_dilated(wrapped[None], kernel, (1, 1, 1), 'VALID', dimen...  213 us
    unnamed x2, waiting for transfers between devices  121 us
    unnamed x1, blocking collectives  62.8 us
    conv_general_dilated x5, local copies, waits for them, and re-layouts, shards(): lax.conv_general_dilated(wrapped[None], kernel, (1, 1, 1), 'VALID', dimen...  42.6 us
    all_gather x1, blocking collectives, shards(): lax.all_gather(mixed_modes, 'gx', axis=2, tiled=True)  32.1 us
    all_to_all x1, starting transfers between devices, shards(): lax.all_to_all(jnp.stack([x_inverse] * lax.axis_size('gy')), 'gy', 0, 0)  27.5 us
  transfers between devices with their start and end apart: 6, of which 3 were waited for; matrix products, arithmetic and copies ran while one was open for 45% of the time, Pallas kernels for 0%

profile of v1, /device:TPU:1, one launch (start us, length us, event | category | flops | bytes accessed | tf_op | source)
XLA Modules:
  0.0 597.2 jit_solution(881018344899034786)
XLA Ops:
  6.6 2.2 convolution_bitcast_fusion
  8.8 1.3 fusion.180
  10.1 2.1 copy.52
  14.9 1.8 fusion.13
  16.7 2.0 copy.54
  22.3 2.1 collective-permute-start
  24.4 5.4 collective-permute-start.1
  33.3 7.2 %collective-permute-start.2 = (f32[16,10,1,128]{3,0,2,1:T(8,128)S(1)}, f32[16,10,1,128]{3,0,2,1:T(8,128)S(1)}, u32[]{:S(2)}, u32[]{:S(2)}) collective-permute-start(f32[16,10,1,128]{3,0,2,1:T(8,128)S(1)} %get-tuple-element.13), channel_id=1, source_target_pairs={{0,1},{1,2},{2,3},{3,4},{4,5},{5,6},{6,7},{7,8},{8,9},{9,10},{10,1... | collective-permute-start | bytes 245768 | tf_op jit(solution)/shard_map/ppermute | solution.py:20
  40.7 1.4 collective-permute-done.2
  42.1 7.3 %collective-permute-done.3 = f32[16,10,1,128]{3,0,2,1:T(8,128)S(1)} collective-permute-done((f32[16,10,1,128]{3,0,2,1:T(8,128)S(1)}, f32[16,10,1,128]{3,0,2,1:T(8,128)S(1)}, u32[]{:S(2)}, u32[]{:S(2)}) %collective-permute-start.3) | collective-permute-done | bytes 81952 | tf_op jit(solution)/shard_map/ppermute | solution.py:21
  49.9 1.2 maximum_bitcast_fusion
  51.5 6.6 %reshape.54 = f32[16,10,18,1,8,17]{5,4,0,2,1,3:T(8,128)} reshape(f32[16,10,18,1,136]{4,0,2,1,3:T(8,128)S(1)} %pad) | data formatting | bytes 3133440 | tf_op jit(solution)/shard_map/conv_general_dilated | solution.py:67
  58.0 15.0 %copy.48 = f32[16,10,18,1,8,17]{0,4,5,2,1,3:T(8,128)} copy(f32[16,10,18,1,8,17]{5,4,0,2,1,3:T(8,128)} %reshape.54) | data formatting | bytes 3133440 | tf_op jit(solution)/shard_map/conv_general_dilated | solution.py:67
  73.0 1.5 slice.80
  74.6 9.6 %fusion.198 = f32[16,10,18,8,19]{0,3,4,2,1:T(8,128)} fusion(f32[16,10,18,1,7,2]{0,4,5,2,1,3:T(8,128)S(1)} %slice.80, f32[16,10,18,1,8,17]{0,4,5,2,1,3:T(8,128)} %copy.48), kind=kLoop, calls=%fused_computation.1.clone.clone.clone.clone.1 | loop fusion | flops 1313280 | bytes 3479040 | tf_op jit(solution)/shard_map/conv_general_dilated | solution.py:67
  84.1 121.1 %all-reduce.4.cloned.1.call-done = f32[16,8,2,288]{3,1,0,2:T(8,128)} async-done(((f32[16,8,2,288]{3,1,0,2:T(8,128)}), f32[16,8,2,288]{3,1,0,2:T(8,128)}) %all-reduce.4.cloned.1.call-update) | async-done | bytes 294928
  205.2 1.4 fusion.38
  206.6 1.4 fusion.15
  208.1 1.4 fusion.39
  209.5 1.4 fusion.14
  211.1 62.8 %all-reduce.1 = f32[16,2,432]{2,0,1:T(8,128)S(1)} all-reduce(f32[16,2,432]{2,0,1:T(8,128)S(1)} %pad_maximum_fusion.3), channel_id=3, replica_groups=mesh['gx'=16,'gy'=16] {'gx'}, use_global_device_ids=true, to_apply=%region_1.2.clone | all-reduce | flops 13824 | bytes 110592
  274.2 32.1 %all_gather.3 = f32[16,2,432]{0,1,2:T(2,128)S(1)} all-gather(f32[16,2,27]{0,1,2:T(2,128)S(1)} %copy.58), channel_id=1, replica_groups=mesh['gx'=16,'gy'=16] {'gx'}, dimensions={2}, use_global_device_ids=true | all-gather | bytes 58752 | tf_op jit(solution)/shard_map/all_gather | solution.py:110
  308.7 2.7 reshape.85
  311.4 27.5 %all-to-all-start = ((f32[16,1,4608]{2,1,0:T(1,128)}), f32[16,1,4608]{2,1,0:T(1,128)S(1)}, u32[]{:S(2)}, u32[]{:S(2)}) async-start(f32[16,1,4608]{2,1,0:T(1,128)} %reshape.85), calls=%async_computation | async-start | bytes 589824 | tf_op jit(solution)/shard_map/all_to_all | solution.py:116
  338.9 213.4 %broadcast_select_fusion = f32[8,16,8,17,16]{4,2,3,1,0:T(8,128)} fusion(pred[8,17]{0,1:T(8,128)(4,1)S(1)} %copy-done.7, f32[3,3,3,16,16]{4,3,2,1,0:T(8,128)S(1)} %bitcast.195, f32[16,10,18,8,19]{0,3,4,2,1:T(8,128)} %fusion.198), kind=kOutput, calls=%fused_computation.8 | convolution fusion | flops 1444167680 | bytes 2892936 | tf_op jit(solution)/shard_map/conv_general_dilated | solution.py:67
  552.4 12.5 %copy.98 = f32[8,16,8,17,16]{3,2,1,0,4:T(8,128)} copy(f32[8,16,8,17,16]{4,2,3,1,0:T(8,128)} %broadcast_select_fusion) | data formatting | bytes 2228224 | tf_op jit(solution)/shard_map/conv_general_dilated | solution.py:67
  564.9 7.0 %reshape.78 = f32[8,16,1,136,16]{3,1,0,4,2:T(8,128)} reshape(f32[8,16,8,17,16]{3,2,1,0,4:T(8,128)} %copy.98) | data formatting | bytes 2228224 | tf_op jit(solution)/shard_map/conv_general_dilated | solution.py:67
  572.4 1.3 reduce.8
  573.7 2.4 reshape.86
  576.2 1.2 copy.61
  579.1 2.2 fusion.59
  585.8 4.2 fusion.19
  (77 shorter events, 19.1 us)
Async XLA Ops:
  6.5 198.7 %all-reduce.4.cloned.1.call-start = ((), (), s32[]{:S(2)}) async-start(), calls=%async_computation.1 | async-start | bytes 786432
  20.9 1.3 copy-start
  21.3 8.5 %copy-start.3 = (f32[2,16,16,1,27]{4,3,2,1,0:T(1,128)S(1)}, f32[2,16,16,1,27]{4,3,2,1,0:T(1,128)}, u32[]{:S(2)}) copy-start(f32[2,16,16,1,27]{4,3,2,1,0:T(1,128)} %param.5) | copy-start | bytes 165892
  21.3 8.5 %copy-start.6 = (u32[256]{0:T(256)S(1)}, u32[256]{0:T(256)}, u32[]{:S(2)}) copy-start(u32[256]{0:T(256)} %constant.138) | copy-start | bytes 3076
  21.4 9.1 %copy-start.5 = (u32[256]{0:T(256)S(1)}, u32[256]{0:T(256)}, u32[]{:S(2)}) copy-start(u32[256]{0:T(256)} %constant.142) | copy-start | bytes 3076
  21.4 9.8 %copy-start.4 = (f32[27,16,16]{0,2,1:T(8,128)S(1)}, f32[27,16,16]{0,2,1:T(8,128)}, u32[]{:S(2)}) copy-start(f32[27,16,16]{0,2,1:T(8,128)} %param.4) | copy-start | bytes 82948
  22.3 10.4 %collective-permute-start = (f32[16,1,16,128]{3,0,2,1:T(8,128)S(1)}, f32[16,1,16,128]{3,0,2,1:T(8,128)S(1)}, u32[]{:S(2)}, u32[]{:S(2)}) collective-permute-start(f32[16,1,16,128]{3,0,2,1:T(8,128)S(1)} %copy.110), channel_id=1, source_target_pairs={{0,16},{16,32},{32,48},{48,64},{64,80},{80,96},{96,112},{112,128},... | collective-permute-start | bytes 393224 | tf_op jit(solution)/shard_map/ppermute | solution.py:20
  24.4 8.9 %collective-permute-start.1 = (f32[16,1,16,128]{3,0,2,1:T(8,128)S(1)}, f32[16,1,16,128]{3,0,2,1:T(8,128)S(1)}, u32[]{:S(2)}, u32[]{:S(2)}) collective-permute-start(f32[16,1,16,128]{3,0,2,1:T(8,128)S(1)} %copy.111), channel_id=1, source_target_pairs={{16,0},{32,16},{48,32},{64,48},{80,64},{96,80},{112,96},{128,112},... | collective-permute-start | bytes 393224 | tf_op jit(solution)/shard_map/ppermute | solution.py:21
  33.3 8.7 %collective-permute-start.2 = (f32[16,10,1,128]{3,0,2,1:T(8,128)S(1)}, f32[16,10,1,128]{3,0,2,1:T(8,128)S(1)}, u32[]{:S(2)}, u32[]{:S(2)}) collective-permute-start(f32[16,10,1,128]{3,0,2,1:T(8,128)S(1)} %get-tuple-element.13), channel_id=1, source_target_pairs={{0,1},{1,2},{2,3},{3,4},{4,5},{5,6},{6,7},{7,8},{8,9},{9,10},{10,1... | collective-permute-start | bytes 245768 | tf_op jit(solution)/shard_map/ppermute | solution.py:20
  40.5 8.8 %collective-permute-start.3 = (f32[16,10,1,128]{3,0,2,1:T(8,128)S(1)}, f32[16,10,1,128]{3,0,2,1:T(8,128)S(1)}, u32[]{:S(2)}, u32[]{:S(2)}) collective-permute-start(f32[16,10,1,128]{3,0,2,1:T(8,128)S(1)} %get-tuple-element.14), channel_id=1, source_target_pairs={{1,0},{2,1},{3,2},{4,3},{5,4},{6,5},{7,6},{8,7},{9,8},{10,9},{11,1... | collective-permute-start | bytes 245768 | tf_op jit(solution)/shard_map/ppermute | solution.py:21
  308.7 30.2 %copy-start.7 = (pred[8,17]{0,1:T(8,128)(4,1)S(1)}, pred[8,17]{0,1:T(8,128)(4,1)}, u32[]{:S(2)}) copy-start(pred[8,17]{0,1:T(8,128)(4,1)} %constant.131) | copy-start | bytes 412
  311.4 260.4 %all-to-all-start = ((f32[16,1,4608]{2,1,0:T(1,128)}), f32[16,1,4608]{2,1,0:T(1,128)S(1)}, u32[]{:S(2)}, u32[]{:S(2)}) async-start(f32[16,1,4608]{2,1,0:T(1,128)} %reshape.85), calls=%async_computation | async-start | bytes 589824 | tf_op jit(solution)/shard_map/all_to_all | solution.py:116
  581.8 1.2 copy-start.1
  584.2 1.6 copy-start.2
Sparse Core Ops, SparseCore 0:
  22.3 182.8 all-reduce.3
